TPU v7x, 32 devices: a whole 2x2x4 slice. The times are simulated.
32 devices in a mesh: group: 2 (over x), seq: 8 (over z, y), tensor: 2 (over core).
Axes of the slice: x: 2, y: 2, z: 4, core: 2. Of those that a mesh axis runs over, the one named last changes fastest.
Arguments:
- hidden: bfloat16 [6, 1024, 8192], P('group', 'seq', 'tensor'), parts along dimension 0, may hold values from -64 to 64
- norm_gain: bfloat16 [8192], replicated, may hold values from 0.099609375 to 1.8984375
- w_kv: bfloat16 [8192, 1024], P(None, 'tensor'), may hold values from -0.0625 to 0.0625
- lengths: int32 [6], P('group'), parts along dimension 0, may hold values from 512 to 1024
- page_table: int32 [6, 8], P('group', 'seq'), parts along dimension 0, may hold values from 0 to 63, as said below
Outputs:
- kv_cache: bfloat16 [128, 128, 1024], P(('group', 'seq'), None, 'tensor'), parts along dimension 0
There are 2 independent parts, one for each index of `group`. A program takes and returns all parts, laid end to end along the dimension named above; an argument that names none is the same for every part. Nothing has to cross between parts.
Inputs may be any that keep to these rules, and one draw needn't show every extreme that they name: `page_table`: entries are distinct; page p is held by index p // 8 of seq in its slot p % 8. In every draw some index of seq holds 8 pages whose blocks all start below the window's length, and some index of seq sends all its 3 blocks to that one holder.
All inputs are finite; a program needn't handle non-finite values.
Results may differ from a plain program's by a relative error of at most 0.0049.
Values may be sent and summed in bfloat16 or wider, within the bound.
No kernel may reach another device: no remote copies, remote signals or barrier semaphores. Data moves between devices by JAX's collectives and lax.ppermute only.
A program may use at most 128 MiB of HBM per device.

v0:
```python
import functools

import jax
import jax.numpy as jnp
from jax import lax
from jax.experimental import pallas as pl
from jax.experimental.pallas import tpu as pltpu
from jax.sharding import PartitionSpec as P


HD = 128
BLOCK = 128
SLOTS = 8
LABEL_ROWS = 8
PIECES = 2
DEPTH = 512
VMEM_LIMIT = 16 << 20


epsilon = 1e-05
rope_base = 500000.0


def rotary_tables(positions):
    half_dim = HD // 2
    inv_freq = rope_base ** (-2.0 * jnp.arange(half_dim, dtype=jnp.float32) / HD)
    angles = positions.astype(jnp.float32)[:, None] * inv_freq[None, :]
    cosine = jnp.cos(angles)
    sine = jnp.sin(angles)
    return jnp.concatenate([cosine, cosine], axis=-1), jnp.concatenate([-sine, sine], axis=-1)


VMEM = pl.BlockSpec(memory_space=pltpu.VMEM)
SMEM = pl.BlockSpec(memory_space=pltpu.SMEM)
ANY = pl.BlockSpec(memory_space=pl.ANY)
HBM = pl.BlockSpec(memory_space=pltpu.HBM)


def near(array):
    return pltpu.with_memory_space_constraint(array, pltpu.VMEM)


def far_away(array):
    return pltpu.with_memory_space_constraint(array, pltpu.HBM)


def lane_squares(x):
    wide = x.astype(jnp.float32)
    wide = wide * wide
    total = wide[:, :128]
    for c in range(1, x.shape[1] // 128):
        total += wide[:, c * 128 : (c + 1) * 128]
    return total


def scaled_by(x, gain_ref, row):
    parts = []
    for c in range(x.shape[1] // 128):
        gain = gain_ref[pl.ds(row + c, 1), :]
        wide = x[:, c * 128 : (c + 1) * 128].astype(jnp.float32) * gain
        parts.append(wide.astype(jnp.bfloat16))
    return jnp.concatenate(parts, axis=1)


def first_half_kernel(x_hbm, g_hbm, w_hbm, acc_ref, sq_ref, far_ref, gain, g_buf, x_buf, w_buf, x_sem, w_sem, sems):
    width = x_hbm.shape[1]
    steps = width // DEPTH
    side = lax.axis_index("tensor")
    near_row = pl.multiple_of(side * width, width)
    far_row = pl.multiple_of((1 - side) * width, width)
    copies = []
    for k in range(steps):
        span = slice(k * DEPTH, (k + 1) * DEPTH)
        copies.append(
            (
                pltpu.make_async_copy(x_hbm.at[:, span], x_buf.at[:, span], x_sem.at[k]),
                pltpu.make_async_copy(
                    w_hbm.at[pl.ds(near_row + k * DEPTH, DEPTH)], w_buf.at[span], w_sem.at[k]
                ),
            )
        )
    far = pltpu.make_async_copy(w_hbm.at[pl.ds(far_row, width)], far_ref, sems.at[0])
    gain_copy = pltpu.make_async_copy(g_hbm, g_buf, sems.at[1])
    gain_copy.start()
    for x_copy, w_copy in copies:
        x_copy.start()
        w_copy.start()
    far.start()
    gain_copy.wait()
    gain[...] = g_buf[...].astype(jnp.float32)
    for k in range(steps):
        for copy in copies[k]:
            copy.wait()
        span = slice(k * DEPTH, (k + 1) * DEPTH)
        x = x_buf[:, span]
        scaled = scaled_by(x, gain, side * (width // 128) + k * (DEPTH // 128))
        part = jnp.dot(scaled, w_buf[span], preferred_element_type=jnp.float32)
        squares = lane_squares(x)
        if k == 0:
            acc_ref[...] = part
            sq_ref[...] = squares
        else:
            acc_ref[...] += part
            sq_ref[...] += squares
    far.wait()


def first_half(x, gain, w):
    rows, width = x.shape
    cols = w.shape[1]
    steps = width // DEPTH
    return pl.pallas_call(
        first_half_kernel,
        in_specs=[HBM, HBM, HBM],
        out_specs=[VMEM, VMEM, VMEM, VMEM],
        out_shape=[
            pltpu.VMEM((rows, cols), jnp.float32),
            pltpu.VMEM((rows, 128), jnp.float32),
            pltpu.VMEM((width, cols), jnp.bfloat16),
            pltpu.VMEM(gain.shape, jnp.float32),
        ],
        scratch_shapes=[
            pltpu.VMEM(gain.shape, jnp.bfloat16),
            pltpu.VMEM((rows, width), jnp.bfloat16),
            pltpu.VMEM((width, cols), jnp.bfloat16),
            pltpu.SemaphoreType.DMA((steps,)),
            pltpu.SemaphoreType.DMA((steps,)),
            pltpu.SemaphoreType.DMA((2,)),
        ],
        compiler_params=pltpu.CompilerParams(vmem_limit_bytes=VMEM_LIMIT),
        cost_estimate=pl.CostEstimate(
            flops=2 * rows * width * cols,
            bytes_accessed=2 * (rows * width + 2 * width * cols) + 4 * rows * cols,
            transcendentals=0,
        ),
        name="first_half",
    )(far_away(x), far_away(gain), far_away(w))


def labels_of(page_ref):
    lane = lax.broadcasted_iota(jnp.int32, (LABEL_ROWS, 128), 1)
    tile = jnp.zeros((LABEL_ROWS, 128), jnp.int32)
    for b in range(page_ref.shape[0]):
        tile = jnp.where(lane == 2 * b, page_ref[b] // SLOTS, tile)
        tile = jnp.where(lane == 2 * b + 1, page_ref[b] % SLOTS, tile)
    return tile.astype(jnp.float32).astype(jnp.bfloat16)


def second_half_kernel(group, piece, len_ref, page_ref, x_ref, g_ref, w_ref, acc_in, norm_in, cos_ref, sin_ref, *refs):
    rows, width = x_ref.shape
    seqs = len_ref.shape[0]
    cols = acc_in.shape[1] // PIECES
    tiles = cols // 128
    side = lax.axis_index("tensor")
    own_index = lax.axis_index("seq")
    lanes = slice(piece * cols, (piece + 1) * cols)
    acc = acc_in[:, lanes]
    squares = norm_in[...]
    for k in range(width // DEPTH):
        span = slice(k * DEPTH, (k + 1) * DEPTH)
        x = x_ref[:, span]
        scaled = scaled_by(x, g_ref, (1 - side) * (width // 128) + k * (DEPTH // 128))
        acc += jnp.dot(scaled, w_ref[span, lanes], preferred_element_type=jnp.float32)
        if piece == 0:
            squares += lane_squares(x)
    if piece == 0:
        early, stage, inv_ref = refs[:3]
        total = jnp.sum(squares, axis=-1, keepdims=True)
        inv = jnp.broadcast_to(lax.rsqrt(total / (2 * width) + epsilon), squares.shape)
        inv_ref[...] = inv
    else:
        before, early = refs[:2]
        outs = refs[2 : 2 + group]
        stage = refs[2 + group]
        inv = squares
    per_seq = rows // seqs
    row = own_index * per_seq + lax.broadcasted_iota(jnp.int32, (per_seq, HD), 0)
    cosine = cos_ref[...]
    sine = sin_ref[...]
    chunk = BLOCK // group
    per = per_seq // BLOCK
    for s in range(seqs):
        living = row < len_ref[s]
        band = slice(s * per_seq, (s + 1) * per_seq)
        inv_s = inv[band]
        for tile in range(0, tiles, 2):
            keys = acc[band, tile * HD : (tile + 1) * HD] * inv_s
            values = acc[band, (tile + 1) * HD : (tile + 2) * HD] * inv_s
            rotated = keys * cosine + pltpu.roll(keys, HD // 2, 1) * sine
            rotated = jnp.where(living, rotated, 0.0).astype(jnp.bfloat16)
            values = jnp.where(living, values, 0.0).astype(jnp.bfloat16)
            for b in range(per):
                part = slice(b * BLOCK, (b + 1) * BLOCK)
                stage[s * per + b, tile] = rotated[part]
                stage[s * per + b, tile + 1] = values[part]
    own = lax.rem(own_index, group)
    blocks = stage.shape[0]

    def copy_chunks(out, source, first, stride, member):
        start = pl.multiple_of((own ^ member) * chunk, chunk)
        for b in range(blocks):
            for tile in range(tiles):
                at = (b * stride + first + tile) * chunk
                out[at : at + chunk, :] = source[b, tile, pl.ds(start, chunk), :]

    copy_chunks(early, stage, 0, tiles, 0)
    if piece == 0:
        early[-LABEL_ROWS:, :] = labels_of(page_ref)
    else:
        for m in range(group):
            copy_chunks(outs[m], before, 0, PIECES * tiles, m)
            copy_chunks(outs[m], stage, tiles, PIECES * tiles, m)
            outs[m][-LABEL_ROWS:, :] = labels_of(page_ref)


def second_half(lengths, pages, x, gain, w, acc, norm, cosine, sine, group, before=None):
    rows, width = x.shape
    piece = 0 if before is None else 1
    cols = w.shape[1] // PIECES
    blocks = rows // BLOCK
    tiles = cols // 128
    half = blocks * tiles * (BLOCK // group)
    stage = pltpu.VMEM((blocks, tiles, BLOCK, 128), jnp.bfloat16)
    scratch = []
    operands = [lengths, pages, near(x), near(gain), near(w), near(acc), near(norm), cosine, sine]
    if piece == 0:
        out_shape = [
            pltpu.VMEM((half + LABEL_ROWS, 128), jnp.bfloat16),
            stage,
            pltpu.VMEM((rows, 128), jnp.float32),
        ]
    else:
        operands.append(near(before))
        out_shape = [pltpu.VMEM((half, 128), jnp.bfloat16)]
        out_shape += [pltpu.VMEM((PIECES * half + LABEL_ROWS, 128), jnp.bfloat16)] * group
        scratch.append(stage)
    return pl.pallas_call(
        functools.partial(second_half_kernel, group, piece),
        in_specs=[SMEM] * 2 + [VMEM] * (len(operands) - 2),
        out_specs=[VMEM] * len(out_shape),
        out_shape=out_shape,
        scratch_shapes=scratch,
        compiler_params=pltpu.CompilerParams(vmem_limit_bytes=VMEM_LIMIT),
        cost_estimate=pl.CostEstimate(
            flops=2 * rows * width * cols,
            bytes_accessed=2 * (rows * width + width * cols) + 4 * rows * cols,
            transcendentals=0,
        ),
    )(*operands)


def route_kernel(cuts, group, blocks, *refs):
    count = sum(cuts)
    parts = refs[:count]
    outs = refs[count : count + group]
    pool, label_buf, label_ref, table, sem = refs[count + group :]
    _, tiles, chunk, _ = pool.shape
    at = 0
    for k, cut in enumerate(cuts):
        label_buf[k : k + 1, :] = parts[at][-LABEL_ROWS:, :].astype(jnp.float32)[:1].astype(jnp.int32)
        at += cut
    copy = pltpu.make_async_copy(label_buf, label_ref, sem)
    copy.start()
    at = 0
    for k, cut in enumerate(cuts):
        span = tiles // cut
        for piece in range(cut):
            for b in range(blocks):
                for tile in range(span):
                    row = (b * span + tile) * chunk
                    pool[k * blocks + b, piece * span + tile] = parts[at + piece][row : row + chunk, :]
        at += cut
    for i in range(group * SLOTS):
        table[i] = -1
    copy.wait()
    own_index = lax.axis_index("seq")
    for k in range(len(cuts)):
        for b in range(blocks):
            member = label_ref[k, 2 * b] ^ own_index
            slot = label_ref[k, 2 * b + 1]

            @pl.when(member < group)
            def _():
                table[member * SLOTS + slot] = k * blocks + b

    for m in range(group):
        for s in range(SLOTS):
            index = table[m * SLOTS + s]
            got = pool[jnp.maximum(index, 0)]
            outs[m][s] = jnp.where(index >= 0, got, jnp.zeros_like(got))


def route(parts, group, blocks):
    cuts = tuple(len(part) for part in parts)
    flat = [near(array) for part in parts for array in part]
    chunk = BLOCK // group
    tiles = (parts[0][0].shape[0] - LABEL_ROWS) // (blocks * chunk)
    count = len(cuts)
    return pl.pallas_call(
        functools.partial(route_kernel, cuts, group, blocks),
        in_specs=[VMEM] * len(flat),
        out_specs=[VMEM] * group,
        out_shape=[pltpu.VMEM((SLOTS, tiles, chunk, 128), jnp.bfloat16)] * group,
        scratch_shapes=[
            pltpu.VMEM((count * blocks, tiles, chunk, 128), jnp.bfloat16),
            pltpu.VMEM((count, 128), jnp.int32),
            pltpu.SMEM((count, 128), jnp.int32),
            pltpu.SMEM((group * SLOTS,), jnp.int32),
            pltpu.SemaphoreType.DMA,
        ],
        compiler_params=pltpu.CompilerParams(vmem_limit_bytes=VMEM_LIMIT),
        cost_estimate=pl.CostEstimate(
            flops=0,
            bytes_accessed=256 * (count * blocks + group * SLOTS) * tiles * chunk,
            transcendentals=0,
        ),
        name="route",
    )(*flat)


def join_kernel(*refs):
    out, buf, sems = refs[-3:]
    parts = refs[:-3]
    group = len(parts)
    slots, tiles, chunk, _ = parts[0].shape
    own = lax.rem(lax.axis_index("seq"), group)
    copies = []
    for s in range(slots):
        for m in range(group):
            start = pl.multiple_of((own ^ m) * chunk, chunk)
            for tile in range(tiles):
                buf[s, pl.ds(start, chunk), tile * 128 : (tile + 1) * 128] = parts[m][s, tile]
        copy = pltpu.make_async_copy(buf.at[s], out.at[s], sems.at[s])
        copy.start()
        copies.append(copy)
    for copy in copies:
        copy.wait()


def join(parts):
    slots, tiles, _, _ = parts[0].shape
    shape = (slots, BLOCK, tiles * 128)
    return pl.pallas_call(
        join_kernel,
        in_specs=[VMEM] * len(parts),
        out_specs=ANY,
        out_shape=jax.ShapeDtypeStruct(shape, jnp.bfloat16),
        scratch_shapes=[pltpu.VMEM(shape, jnp.bfloat16), pltpu.SemaphoreType.DMA((slots,))],
        compiler_params=pltpu.CompilerParams(vmem_limit_bytes=VMEM_LIMIT),
        cost_estimate=pl.CostEstimate(
            flops=0, bytes_accessed=4 * slots * BLOCK * tiles * 128, transcendentals=0
        ),
        name="join",
    )(*[near(part) for part in parts])


def per_device(seq_size, hidden, norm_gain, w_kv, lengths, page_table):
    seq_count, row_count, local_width = hidden.shape
    group = min(4, seq_size)
    own_index = lax.axis_index("seq").astype(jnp.int32)
    flat = hidden.reshape(seq_count * row_count, local_width)
    other = lax.ppermute(flat, "tensor", [(0, 1), (1, 0)])

    def swap(array, k):
        return lax.ppermute(array, "seq", [(i, i ^ k) for i in range(seq_size)])

    positions = own_index * row_count + jnp.arange(row_count, dtype=jnp.int32)
    cosine, sine = rotary_tables(positions)
    gain = norm_gain.reshape(-1, 128)
    pages = page_table.reshape(-1)
    flat, cosine, sine = lax.optimization_barrier((flat, cosine, sine))
    acc, squares, far, gain = first_half(flat, gain, w_kv)
    shared = (cosine, sine, group)
    early, before, inv = second_half(lengths, pages, other, gain, far, acc, squares, *shared)
    parts = {}
    if seq_size > group:
        parts[group] = [swap(early, group)]
    late, *outs = second_half(lengths, pages, other, gain, far, acc, inv, *shared, before)
    for k in range(group + 1, seq_size):
        parts[k] = [swap(outs[k % group], k)]
    if seq_size > group:
        parts[group].append(swap(late, group))
    for k in range(1, group):
        parts[k] = [swap(outs[k], k)]
    parts[0] = [outs[0]]
    sent = route([parts[k] for k in range(seq_size)], group, seq_count * row_count // BLOCK)
    placed = [sent[0]]
    for m in range(1, group):
        placed.append(swap(sent[m], m))
    return join(placed)


def solution(mesh):
    placed = (P("group", "seq", "tensor"), P(), P(None, "tensor"), P("group"), P("group", "seq"))

    def body(*operands):
        return per_device(mesh.shape["seq"], *operands)

    return jax.shard_map(
        body,
        mesh=mesh,
        in_specs=placed,
        out_specs=P(("group", "seq"), None, "tensor"),
        check_vma=False,
    )
```

profile of v0, /device:TPU:0, one launch (start us, length us, event | category | flops | bytes accessed | tf_op | source)
XLA Modules:
  0.0 53.5 jit_solution(2479267620889523138)
XLA Ops:
  0.0 0.5 collective-permute-start
  0.5 0.3 fusion
  0.8 0.1 pad_maximum_fusion
  1.0 5.0 %first_half.1 = (f32[384,512]{1,0:T(8,128)S(1)}, f32[384,128]{1,0:T(8,128)S(1)}, bf16[4096,512]{1,0:T(8,128)(2,1)S(1)}, f32[64,128]{1,0:T(8,128)S(1)}) custom-call(bf16[384,4096]{1,0:T(8,128)(2,1)} %bitcast.6, bf16[64,128]{1,0:T(8,128)(2,1)} %bitcast.7, bf16[8192,512]{1,0:T(8,128)(2,1)} %w_hbm.1), custom_call_target="tpu_custom_call" | custom-call | flops 1610612736 | bytes 12320768 | tf_op jit(solution)/shard_map/first_half/pallas_call | solution.py:112
  6.0 0.0 collective-permute-done.x_ref
  6.0 1.8 %shard_map.55 = (bf16[200,128]{1,0:T(8,128)(2,1)S(1)}, bf16[3,2,128,128]{3,2,1,0:T(8,128)(2,1)S(1)}, f32[384,128]{1,0:T(8,128)S(1)}) custom-call(s32[3]{0:T(128)S(1)} %copy-done, s32[3]{0:T(128)S(1)} %bitcast.3, bf16[384,4096]{1,0:T(8,128)(2,1)S(1)} %collective-permute-done.x_ref, f32[64,128]{1,0:T(8,128)S(1)} %get-tuple-element.25.g_ref, ...), custom_call_target="tpu_custom_call" | custom-call | flops 805306368 | bytes 5636096 | tf_op jit(solution)/shard_map/pallas_call | solution.py:237
  7.8 1.6 %shard_map.56 = (bf16[192,128]{1,0:T(8,128)(2,1)S(1)}, bf16[392,128]{1,0:T(8,128)(2,1)S(1)}, bf16[392,128]{1,0:T(8,128)(2,1)S(1)}, bf16[392,128]{1,0:T(8,128)(2,1)S(1)}, bf16[392,128]{1,0:T(8,128)(2,1)S(1)}) custom-call(s32[3]{0:T(128)S(1)} %copy-done, s32[3]{0:T(128)S(1)} %bitcast.4, bf16[384,4096]{1,0:T(8,128)(2,1)S(1)} %collective-permute-done.x_ref, ...), custom_call_target="tpu_custom_call" | custom-call | flops 805306368 | bytes 5636096 | tf_op jit(solution)/shard_map/pallas_call | solution.py:237
  9.4 5.0 %collective-permute-start.6 = (bf16[392,128]{1,0:T(8,128)(2,1)S(1)}, bf16[392,128]{1,0:T(8,128)(2,1)S(1)}, u32[]{:S(2)}, u32[]{:S(2)}) collective-permute-start(bf16[392,128]{1,0:T(8,128)(2,1)S(1)} %get-tuple-element.34), channel_id=1, source_target_pairs={{0,10},{2,8},{4,14},{6,12},{8,2},{10,0},{12,6},{14,4},{1,11},{3,9}... | collective-permute-start | bytes 301064 | tf_op jit(solution)/shard_map/ppermute | solution.py:365
  14.4 0.3 collective-permute-start.4
  14.7 2.6 %collective-permute-start.5 = (bf16[192,128]{1,0:T(8,128)(2,1)S(1)}, bf16[192,128]{1,0:T(8,128)(2,1)S(1)}, u32[]{:S(2)}, u32[]{:S(2)}) collective-permute-start(bf16[192,128]{1,0:T(8,128)(2,1)S(1)} %get-tuple-element.38), channel_id=1, source_target_pairs={{0,8},{2,10},{4,12},{6,14},{8,0},{10,2},{12,4},{14,6},{1,9},{3,11}... | collective-permute-start | bytes 147464 | tf_op jit(solution)/shard_map/ppermute | solution.py:365
  17.3 0.5 collective-permute-start.1
  17.8 1.4 %collective-permute-start.7 = (bf16[392,128]{1,0:T(8,128)(2,1)S(1)}, bf16[392,128]{1,0:T(8,128)(2,1)S(1)}, u32[]{:S(2)}, u32[]{:S(2)}) collective-permute-start(bf16[392,128]{1,0:T(8,128)(2,1)S(1)} %get-tuple-element.35), channel_id=1, source_target_pairs={{0,12},{2,14},{4,8},{6,10},{8,4},{10,6},{12,0},{14,2},{1,13},{3,15... | collective-permute-start | bytes 301064 | tf_op jit(solution)/shard_map/ppermute | solution.py:365
  19.2 7.8 %collective-permute-done.5.refs_5_ = bf16[192,128]{1,0:T(8,128)(2,1)S(1)} collective-permute-done((bf16[192,128]{1,0:T(8,128)(2,1)S(1)}, bf16[192,128]{1,0:T(8,128)(2,1)S(1)}, u32[]{:S(2)}, u32[]{:S(2)}) %collective-permute-start.5) | collective-permute-done | bytes 49184 | tf_op jit(solution)/shard_map/ppermute | solution.py:365
  27.0 2.7 %collective-permute-start.8 = (bf16[392,128]{1,0:T(8,128)(2,1)S(1)}, bf16[392,128]{1,0:T(8,128)(2,1)S(1)}, u32[]{:S(2)}, u32[]{:S(2)}) collective-permute-start(bf16[392,128]{1,0:T(8,128)(2,1)S(1)} %get-tuple-element.36), channel_id=1, source_target_pairs={{0,14},{2,12},{4,10},{6,8},{8,6},{10,4},{12,2},{14,0},{1,15},{3,13... | collective-permute-start | bytes 301064 | tf_op jit(solution)/shard_map/ppermute | solution.py:365
  29.7 2.1 %collective-permute-start.3 = (bf16[392,128]{1,0:T(8,128)(2,1)S(1)}, bf16[392,128]{1,0:T(8,128)(2,1)S(1)}, u32[]{:S(2)}, u32[]{:S(2)}) collective-permute-start(bf16[392,128]{1,0:T(8,128)(2,1)S(1)} %get-tuple-element.36), channel_id=1, source_target_pairs={{0,6},{2,4},{4,2},{6,0},{8,14},{10,12},{12,10},{14,8},{1,7},{3,5},... | collective-permute-start | bytes 301064 | tf_op jit(solution)/shard_map/ppermute | solution.py:365
  31.8 3.7 %collective-permute-done.8.refs_8_ = bf16[392,128]{1,0:T(8,128)(2,1)S(1)} collective-permute-done((bf16[392,128]{1,0:T(8,128)(2,1)S(1)}, bf16[392,128]{1,0:T(8,128)(2,1)S(1)}, u32[]{:S(2)}, u32[]{:S(2)}) %collective-permute-start.8) | collective-permute-done | bytes 100384 | tf_op jit(solution)/shard_map/ppermute | solution.py:365
  35.5 1.2 %collective-permute-done.3.refs_3_ = bf16[392,128]{1,0:T(8,128)(2,1)S(1)} collective-permute-done((bf16[392,128]{1,0:T(8,128)(2,1)S(1)}, bf16[392,128]{1,0:T(8,128)(2,1)S(1)}, u32[]{:S(2)}, u32[]{:S(2)}) %collective-permute-start.3) | collective-permute-done | bytes 100384 | tf_op jit(solution)/shard_map/ppermute | solution.py:365
  36.7 0.9 %route.1 = (bf16[8,4,32,128]{3,2,1,0:T(8,128)(2,1)S(1)}, bf16[8,4,32,128]{3,2,1,0:T(8,128)(2,1)S(1)}, bf16[8,4,32,128]{3,2,1,0:T(8,128)(2,1)S(1)}, bf16[8,4,32,128]{3,2,1,0:T(8,128)(2,1)S(1)}) custom-call(bf16[392,128]{1,0:T(8,128)(2,1)S(1)} %get-tuple-element.33.refs_0_, bf16[392,128]{1,0:T(8,128)(2,1)S(1)} %collective-permute-done.1.refs_1_, ...), custom_call_target="tpu_custom_call" | custom-call | bytes 1835008 | tf_op jit(solution)/shard_map/route/pallas_call | solution.py:299
  37.6 1.6 %collective-permute-start.9 = (bf16[8,4,32,128]{3,2,1,0:T(8,128)(2,1)S(1)}, bf16[8,4,32,128]{3,2,1,0:T(8,128)(2,1)S(1)}, u32[]{:S(2)}, u32[]{:S(2)}) collective-permute-start(bf16[8,4,32,128]{3,2,1,0:T(8,128)(2,1)S(1)} %get-tuple-element.40), channel_id=1, source_target_pairs={{0,2},{2,0},{4,6},{6,4},{8,10},{10,8},{12,14},{14,12},{1,3},{3,1},... | collective-permute-start | bytes 786440 | tf_op jit(solution)/shard_map/ppermute | solution.py:365
  39.2 2.0 %collective-permute-start.11 = (bf16[8,4,32,128]{3,2,1,0:T(8,128)(2,1)S(1)}, bf16[8,4,32,128]{3,2,1,0:T(8,128)(2,1)S(1)}, u32[]{:S(2)}, u32[]{:S(2)}) collective-permute-start(bf16[8,4,32,128]{3,2,1,0:T(8,128)(2,1)S(1)} %get-tuple-element.42), channel_id=1, source_target_pairs={{0,6},{2,4},{4,2},{6,0},{8,14},{10,12},{12,10},{14,8},{1,7},{3,5},... | collective-permute-start | bytes 786440 | tf_op jit(solution)/shard_map/ppermute | solution.py:365
  41.2 4.8 %collective-permute-done.9.refs_1_ = bf16[8,4,32,128]{3,2,1,0:T(8,128)(2,1)S(1)} collective-permute-done((bf16[8,4,32,128]{3,2,1,0:T(8,128)(2,1)S(1)}, bf16[8,4,32,128]{3,2,1,0:T(8,128)(2,1)S(1)}, u32[]{:S(2)}, u32[]{:S(2)}) %collective-permute-start.9) | collective-permute-done | bytes 262176 | tf_op jit(solution)/shard_map/ppermute | solution.py:365
  46.0 2.4 %collective-permute-done.10.refs_2_ = bf16[8,4,32,128]{3,2,1,0:T(8,128)(2,1)S(1)} collective-permute-done((bf16[8,4,32,128]{3,2,1,0:T(8,128)(2,1)S(1)}, bf16[8,4,32,128]{3,2,1,0:T(8,128)(2,1)S(1)}, u32[]{:S(2)}, u32[]{:S(2)}) %collective-permute-start.10) | collective-permute-done | bytes 262176 | tf_op jit(solution)/shard_map/ppermute | solution.py:365
  48.4 4.1 %collective-permute-done.11.refs_3_ = bf16[8,4,32,128]{3,2,1,0:T(8,128)(2,1)S(1)} collective-permute-done((bf16[8,4,32,128]{3,2,1,0:T(8,128)(2,1)S(1)}, bf16[8,4,32,128]{3,2,1,0:T(8,128)(2,1)S(1)}, u32[]{:S(2)}, u32[]{:S(2)}) %collective-permute-start.11) | collective-permute-done | bytes 262176 | tf_op jit(solution)/shard_map/ppermute | solution.py:365
  52.5 1.1 %join.1 = bf16[8,128,512]{2,1,0:T(8,128)(2,1)} custom-call(bf16[8,4,32,128]{3,2,1,0:T(8,128)(2,1)S(1)} %get-tuple-element.39.refs_0_, bf16[8,4,32,128]{3,2,1,0:T(8,128)(2,1)S(1)} %collective-permute-done.9.refs_1_, bf16[8,4,32,128]{3,2,1,0:T(8,128)(2,1)S(1)} %collective-permute-done.10.refs_2_, bf16[8,4,32,128]{3,2,1,0:T(8,128)(2,1)S(1)} %collective-permute-done.11.refs_3_), custom_call_target="tpu_custom_call" | custom-call | bytes 2097152 | tf_op jit(solution)/shard_map/join/pallas_call | solution.py:343
  (13 shorter events, 0.0 us)
Async XLA Ops:
  0.0 6.0 %collective-permute-start = (bf16[384,4096]{1,0:T(8,128)(2,1)}, bf16[384,4096]{1,0:T(8,128)(2,1)S(1)}, u32[]{:S(2)}, u32[]{:S(2)}) collective-permute-start(bf16[384,4096]{1,0:T(8,128)(2,1)} %bitcast.5), channel_id=1, source_target_pairs={{0,1},{1,0},{2,3},{3,2},{4,5},{5,4},{6,7},{7,6},{8,9},{9,8},{10,11... | collective-permute-start | bytes 9437192 | tf_op jit(solution)/shard_map/ppermute | solution.py:362
  0.9 5.1 %copy-start = (s32[3]{0:T(128)S(1)}, s32[3]{0:T(128)}, u32[]{:S(2)}) copy-start(s32[3]{0:T(128)} %len_ref.3) | copy-start | bytes 40
  1.0 5.0 %copy-start.1 = (s32[3,1]{0,1:T(1,128)S(1)}, s32[3,1]{0,1:T(1,128)}, u32[]{:S(2)}) copy-start(s32[3,1]{0,1:T(1,128)} %param.9) | copy-start | bytes 40
  9.4 20.3 %collective-permute-start.6 = (bf16[392,128]{1,0:T(8,128)(2,1)S(1)}, bf16[392,128]{1,0:T(8,128)(2,1)S(1)}, u32[]{:S(2)}, u32[]{:S(2)}) collective-permute-start(bf16[392,128]{1,0:T(8,128)(2,1)S(1)} %get-tuple-element.34), channel_id=1, source_target_pairs={{0,10},{2,8},{4,14},{6,12},{8,2},{10,0},{12,6},{14,4},{1,11},{3,9}... | collective-permute-start | bytes 301064 | tf_op jit(solution)/shard_map/ppermute | solution.py:365
  14.4 12.6 %collective-permute-start.4 = (bf16[200,128]{1,0:T(8,128)(2,1)S(1)}, bf16[200,128]{1,0:T(8,128)(2,1)S(1)}, u32[]{:S(2)}, u32[]{:S(2)}) collective-permute-start(bf16[200,128]{1,0:T(8,128)(2,1)S(1)} %get-tuple-element.37), channel_id=1, source_target_pairs={{0,8},{2,10},{4,12},{6,14},{8,0},{10,2},{12,4},{14,6},{1,9},{3,11}... | collective-permute-start | bytes 153608 | tf_op jit(solution)/shard_map/ppermute | solution.py:365
  14.7 12.3 %collective-permute-start.5 = (bf16[192,128]{1,0:T(8,128)(2,1)S(1)}, bf16[192,128]{1,0:T(8,128)(2,1)S(1)}, u32[]{:S(2)}, u32[]{:S(2)}) collective-permute-start(bf16[192,128]{1,0:T(8,128)(2,1)S(1)} %get-tuple-element.38), channel_id=1, source_target_pairs={{0,8},{2,10},{4,12},{6,14},{8,0},{10,2},{12,4},{14,6},{1,9},{3,11}... | collective-permute-start | bytes 147464 | tf_op jit(solution)/shard_map/ppermute | solution.py:365
  17.3 14.5 %collective-permute-start.1 = (bf16[392,128]{1,0:T(8,128)(2,1)S(1)}, bf16[392,128]{1,0:T(8,128)(2,1)S(1)}, u32[]{:S(2)}, u32[]{:S(2)}) collective-permute-start(bf16[392,128]{1,0:T(8,128)(2,1)S(1)} %get-tuple-element.34), channel_id=1, source_target_pairs={{0,2},{2,0},{4,6},{6,4},{8,10},{10,8},{12,14},{14,12},{1,3},{3,1},... | collective-permute-start | bytes 301064 | tf_op jit(solution)/shard_map/ppermute | solution.py:365
  17.8 14.0 %collective-permute-start.7 = (bf16[392,128]{1,0:T(8,128)(2,1)S(1)}, bf16[392,128]{1,0:T(8,128)(2,1)S(1)}, u32[]{:S(2)}, u32[]{:S(2)}) collective-permute-start(bf16[392,128]{1,0:T(8,128)(2,1)S(1)} %get-tuple-element.35), channel_id=1, source_target_pairs={{0,12},{2,14},{4,8},{6,10},{8,4},{10,6},{12,0},{14,2},{1,13},{3,15... | collective-permute-start | bytes 301064 | tf_op jit(solution)/shard_map/ppermute | solution.py:365
  27.0 4.8 %collective-permute-start.2 = (bf16[392,128]{1,0:T(8,128)(2,1)S(1)}, bf16[392,128]{1,0:T(8,128)(2,1)S(1)}, u32[]{:S(2)}, u32[]{:S(2)}) collective-permute-start(bf16[392,128]{1,0:T(8,128)(2,1)S(1)} %get-tuple-element.35), channel_id=1, source_target_pairs={{0,4},{2,6},{4,0},{6,2},{8,12},{10,14},{12,8},{14,10},{1,5},{3,7},... | collective-permute-start | bytes 301064 | tf_op jit(solution)/shard_map/ppermute | solution.py:365
  27.0 8.5 %collective-permute-start.8 = (bf16[392,128]{1,0:T(8,128)(2,1)S(1)}, bf16[392,128]{1,0:T(8,128)(2,1)S(1)}, u32[]{:S(2)}, u32[]{:S(2)}) collective-permute-start(bf16[392,128]{1,0:T(8,128)(2,1)S(1)} %get-tuple-element.36), channel_id=1, source_target_pairs={{0,14},{2,12},{4,10},{6,8},{8,6},{10,4},{12,2},{14,0},{1,15},{3,13... | collective-permute-start | bytes 301064 | tf_op jit(solution)/shard_map/ppermute | solution.py:365
  29.7 7.0 %collective-permute-start.3 = (bf16[392,128]{1,0:T(8,128)(2,1)S(1)}, bf16[392,128]{1,0:T(8,128)(2,1)S(1)}, u32[]{:S(2)}, u32[]{:S(2)}) collective-permute-start(bf16[392,128]{1,0:T(8,128)(2,1)S(1)} %get-tuple-element.36), channel_id=1, source_target_pairs={{0,6},{2,4},{4,2},{6,0},{8,14},{10,12},{12,10},{14,8},{1,7},{3,5},... | collective-permute-start | bytes 301064 | tf_op jit(solution)/shard_map/ppermute | solution.py:365
  37.6 8.3 %collective-permute-start.9 = (bf16[8,4,32,128]{3,2,1,0:T(8,128)(2,1)S(1)}, bf16[8,4,32,128]{3,2,1,0:T(8,128)(2,1)S(1)}, u32[]{:S(2)}, u32[]{:S(2)}) collective-permute-start(bf16[8,4,32,128]{3,2,1,0:T(8,128)(2,1)S(1)} %get-tuple-element.40), channel_id=1, source_target_pairs={{0,2},{2,0},{4,6},{6,4},{8,10},{10,8},{12,14},{14,12},{1,3},{3,1},... | collective-permute-start | bytes 786440 | tf_op jit(solution)/shard_map/ppermute | solution.py:365
  39.2 9.2 %collective-permute-start.10 = (bf16[8,4,32,128]{3,2,1,0:T(8,128)(2,1)S(1)}, bf16[8,4,32,128]{3,2,1,0:T(8,128)(2,1)S(1)}, u32[]{:S(2)}, u32[]{:S(2)}) collective-permute-start(bf16[8,4,32,128]{3,2,1,0:T(8,128)(2,1)S(1)} %get-tuple-element.41), channel_id=1, source_target_pairs={{0,4},{2,6},{4,0},{6,2},{8,12},{10,14},{12,8},{14,10},{1,5},{3,7},... | collective-permute-start | bytes 786440 | tf_op jit(solution)/shard_map/ppermute | solution.py:365
  39.2 13.2 %collective-permute-start.11 = (bf16[8,4,32,128]{3,2,1,0:T(8,128)(2,1)S(1)}, bf16[8,4,32,128]{3,2,1,0:T(8,128)(2,1)S(1)}, u32[]{:S(2)}, u32[]{:S(2)}) collective-permute-start(bf16[8,4,32,128]{3,2,1,0:T(8,128)(2,1)S(1)} %get-tuple-element.42), channel_id=1, source_target_pairs={{0,6},{2,4},{4,2},{6,0},{8,14},{10,12},{12,10},{14,8},{1,7},{3,5},... | collective-permute-start | bytes 786440 | tf_op jit(solution)/shard_map/ppermute | solution.py:365
where the time goes:
time: 53.7 us; the launch traced here: 53.5 us
  waiting for transfers between devices  24 us (45%)
  starting transfers between devices  18.6 us (35%)
  Pallas kernels  10.4 us (19%)
    ppermute x11, waiting for transfers between devices, swap(): return lax.ppermute(array, 'seq', [(i, i ^ k) for i in range(seq_size)])  24 us
    ppermute x11, starting transfers between devices, swap(): return lax.ppermute(array, 'seq', [(i, i ^ k) for i in range(seq_size)])  18.1 us
    pallas_call x1, Pallas kernels, first_half(): pl.pallas_call(first_half_kernel, in_specs=[HBM, HBM, HBM], out_specs=[VM...  5 us
    pallas_call x2, Pallas kernels, second_half(): pl.pallas_call(functools.partial(second_half_kernel, group, piece), in_sp...  3.39 us
  transfers between devices with their start and end apart: 12, of which 6 were waited for; matrix products, arithmetic and copies ran while one was open for 1% of the time, Pallas kernels for 9%

commit v1 on v0

v1 whole, which is shorter than its diff:
```python
import functools

import jax
import jax.numpy as jnp
from jax import lax
from jax.experimental import pallas as pl
from jax.experimental.pallas import tpu as pltpu
from jax.sharding import PartitionSpec as P


HD = 128
BLOCK = 128
SLOTS = 8
LABEL_ROWS = 8
CUTS = (0, 2, 4)
DEPTH = 512
VMEM_LIMIT = 16 << 20


epsilon = 1e-05
rope_base = 500000.0


def frequencies():
    index = jnp.arange(HD, dtype=jnp.int32).reshape(1, HD) % (HD // 2)
    return rope_base ** (-2.0 * index.astype(jnp.float32) / HD)


VMEM = pl.BlockSpec(memory_space=pltpu.VMEM)
SMEM = pl.BlockSpec(memory_space=pltpu.SMEM)
ANY = pl.BlockSpec(memory_space=pl.ANY)
HBM = pl.BlockSpec(memory_space=pltpu.HBM)


def near(array):
    return pltpu.with_memory_space_constraint(array, pltpu.VMEM)


def far_away(array):
    return pltpu.with_memory_space_constraint(array, pltpu.HBM)


def lane_squares(x):
    wide = x.astype(jnp.float32)
    wide = wide * wide
    total = wide[:, :128]
    for c in range(1, x.shape[1] // 128):
        total += wide[:, c * 128 : (c + 1) * 128]
    return total


def scaled_by(x, gain_ref, row):
    parts = []
    for c in range(x.shape[1] // 128):
        gain = gain_ref[pl.ds(row + c, 1), :]
        wide = x[:, c * 128 : (c + 1) * 128].astype(jnp.float32) * gain
        parts.append(wide.astype(jnp.bfloat16))
    return jnp.concatenate(parts, axis=1)


def first_half_kernel(row_count, x_hbm, g_hbm, w_hbm, freq_ref, acc_ref, sq_ref, far_ref, gain, cos_ref, sin_ref, *scratch):
    g_buf, x_buf, w_buf, x_sem, w_sem, sems = scratch
    width = x_hbm.shape[1]
    steps = width // DEPTH
    side = lax.axis_index("tensor")
    near_row = pl.multiple_of(side * width, width)
    far_row = pl.multiple_of((1 - side) * width, width)
    copies = []
    for k in range(steps):
        span = slice(k * DEPTH, (k + 1) * DEPTH)
        copies.append(
            (
                pltpu.make_async_copy(x_hbm.at[:, span], x_buf.at[:, span], x_sem.at[k]),
                pltpu.make_async_copy(
                    w_hbm.at[pl.ds(near_row + k * DEPTH, DEPTH)], w_buf.at[span], w_sem.at[k]
                ),
            )
        )
    far = pltpu.make_async_copy(w_hbm.at[pl.ds(far_row, width)], far_ref, sems.at[0])
    gain_copy = pltpu.make_async_copy(g_hbm, g_buf, sems.at[1])
    gain_copy.start()
    for x_copy, w_copy in copies:
        x_copy.start()
        w_copy.start()
    far.start()
    first = lax.axis_index("seq") * row_count
    position = first + lax.broadcasted_iota(jnp.int32, cos_ref.shape, 0)
    angle = position.astype(jnp.float32) * freq_ref[...]
    cos_ref[...] = jnp.cos(angle)
    sine = jnp.sin(angle)
    lane = lax.broadcasted_iota(jnp.int32, sine.shape, 1)
    sin_ref[...] = jnp.where(lane < HD // 2, -sine, sine)
    gain_copy.wait()
    gain[...] = g_buf[...].astype(jnp.float32)
    for k in range(steps):
        for copy in copies[k]:
            copy.wait()
        span = slice(k * DEPTH, (k + 1) * DEPTH)
        x = x_buf[:, span]
        scaled = scaled_by(x, gain, side * (width // 128) + k * (DEPTH // 128))
        part = jnp.dot(scaled, w_buf[span], preferred_element_type=jnp.float32)
        squares = lane_squares(x)
        if k == 0:
            acc_ref[...] = part
            sq_ref[...] = squares
        else:
            acc_ref[...] += part
            sq_ref[...] += squares
    far.wait()


def first_half(x, gain, w, freq, row_count):
    rows, width = x.shape
    cols = w.shape[1]
    steps = width // DEPTH
    return pl.pallas_call(
        functools.partial(first_half_kernel, row_count),
        in_specs=[HBM, HBM, HBM, VMEM],
        out_specs=[VMEM] * 6,
        out_shape=[
            pltpu.VMEM((rows, cols), jnp.float32),
            pltpu.VMEM((rows, 128), jnp.float32),
            pltpu.VMEM((width, cols), jnp.bfloat16),
            pltpu.VMEM(gain.shape, jnp.float32),
            pltpu.VMEM((row_count, HD), jnp.float32),
            pltpu.VMEM((row_count, HD), jnp.float32),
        ],
        scratch_shapes=[
            pltpu.VMEM(gain.shape, jnp.bfloat16),
            pltpu.VMEM((rows, width), jnp.bfloat16),
            pltpu.VMEM((width, cols), jnp.bfloat16),
            pltpu.SemaphoreType.DMA((steps,)),
            pltpu.SemaphoreType.DMA((steps,)),
            pltpu.SemaphoreType.DMA((2,)),
        ],
        compiler_params=pltpu.CompilerParams(vmem_limit_bytes=VMEM_LIMIT),
        cost_estimate=pl.CostEstimate(
            flops=2 * rows * width * cols,
            bytes_accessed=2 * (rows * width + 2 * width * cols) + 4 * rows * cols,
            transcendentals=0,
        ),
        name="first_half",
    )(far_away(x), far_away(gain), far_away(w), freq)


def labels_of(page_ref):
    lane = lax.broadcasted_iota(jnp.int32, (LABEL_ROWS, 128), 1)
    tile = jnp.zeros((LABEL_ROWS, 128), jnp.int32)
    for b in range(page_ref.shape[0]):
        tile = jnp.where(lane == 2 * b, page_ref[b] // SLOTS, tile)
        tile = jnp.where(lane == 2 * b + 1, page_ref[b] % SLOTS, tile)
    return tile.astype(jnp.float32).astype(jnp.bfloat16)


def second_half_kernel(group, piece, len_ref, page_ref, x_ref, g_ref, w_ref, acc_in, norm_in, cos_ref, sin_ref, *refs):
    rows, width = x_ref.shape
    seqs = len_ref.shape[0]
    first_tile, last_tile = CUTS[piece], CUTS[piece + 1]
    tiles = last_tile - first_tile
    side = lax.axis_index("tensor")
    own_index = lax.axis_index("seq")
    lanes = slice(first_tile * 128, last_tile * 128)
    acc = acc_in[:, lanes]
    squares = norm_in[...]
    for k in range(width // DEPTH):
        span = slice(k * DEPTH, (k + 1) * DEPTH)
        x = x_ref[:, span]
        scaled = scaled_by(x, g_ref, (1 - side) * (width // 128) + k * (DEPTH // 128))
        acc += jnp.dot(scaled, w_ref[span, lanes], preferred_element_type=jnp.float32)
        if piece == 0:
            squares += lane_squares(x)
    if piece == 0:
        early, stage, inv_ref = refs
        total = jnp.sum(squares, axis=-1, keepdims=True)
        inv = jnp.broadcast_to(lax.rsqrt(total / (2 * width) + epsilon), squares.shape)
        inv_ref[...] = inv
    else:
        before, early = refs[:2]
        outs = refs[2 : 2 + group]
        stage = refs[2 + group]
        inv = squares
    per_seq = rows // seqs
    row = own_index * per_seq + lax.broadcasted_iota(jnp.int32, (per_seq, HD), 0)
    cosine = cos_ref[...]
    sine = sin_ref[...]
    chunk = BLOCK // group
    per = per_seq // BLOCK
    for s in range(seqs):
        living = row < len_ref[s]
        band = slice(s * per_seq, (s + 1) * per_seq)
        inv_s = inv[band]
        for tile in range(tiles):
            made = acc[band, tile * HD : (tile + 1) * HD] * inv_s
            if (first_tile + tile) % 2 == 0:
                made = made * cosine + pltpu.roll(made, HD // 2, 1) * sine
            made = jnp.where(living, made, 0.0).astype(jnp.bfloat16)
            for b in range(per):
                stage[s * per + b, tile] = made[b * BLOCK : (b + 1) * BLOCK]
    own = lax.rem(own_index, group)
    blocks = stage.shape[0]

    def copy_chunks(out, source, first, stride, member):
        start = pl.multiple_of((own ^ member) * chunk, chunk)
        for b in range(blocks):
            for tile in range(source.shape[1]):
                at = (b * stride + first + tile) * chunk
                out[at : at + chunk, :] = source[b, tile, pl.ds(start, chunk), :]

    copy_chunks(early, stage, 0, tiles, 0)
    if piece == 0:
        early[-LABEL_ROWS:, :] = labels_of(page_ref)
    else:
        for m in range(group):
            copy_chunks(outs[m], before, 0, CUTS[-1], m)
            copy_chunks(outs[m], stage, first_tile, CUTS[-1], m)
            outs[m][-LABEL_ROWS:, :] = labels_of(page_ref)


def second_half(lengths, pages, x, gain, w, acc, norm, cosine, sine, group, before=None):
    rows, width = x.shape
    piece = 0 if before is None else 1
    tiles = CUTS[piece + 1] - CUTS[piece]
    blocks = rows // BLOCK
    strip = blocks * (BLOCK // group)
    stage = pltpu.VMEM((blocks, tiles, BLOCK, 128), jnp.bfloat16)
    scratch = []
    operands = [lengths, pages, near(x), near(gain), near(w), near(acc), near(norm), near(cosine), near(sine)]
    if piece == 0:
        out_shape = [
            pltpu.VMEM((tiles * strip + LABEL_ROWS, 128), jnp.bfloat16),
            stage,
            pltpu.VMEM((rows, 128), jnp.float32),
        ]
    else:
        operands.append(near(before))
        out_shape = [pltpu.VMEM((tiles * strip, 128), jnp.bfloat16)]
        out_shape += [pltpu.VMEM((CUTS[-1] * strip + LABEL_ROWS, 128), jnp.bfloat16)] * group
        scratch.append(stage)
    return pl.pallas_call(
        functools.partial(second_half_kernel, group, piece),
        in_specs=[SMEM] * 2 + [VMEM] * (len(operands) - 2),
        out_specs=[VMEM] * len(out_shape),
        out_shape=out_shape,
        scratch_shapes=scratch,
        compiler_params=pltpu.CompilerParams(vmem_limit_bytes=VMEM_LIMIT),
        cost_estimate=pl.CostEstimate(
            flops=2 * rows * width * tiles * 128,
            bytes_accessed=2 * width * (rows + tiles * 128) + 4 * rows * tiles * 128,
            transcendentals=0,
        ),
    )(*operands)


def route_kernel(cuts, group, blocks, *refs):
    count = sum(cuts)
    parts = refs[:count]
    outs = refs[count : count + group]
    pool, label_buf, label_ref, table, sem = refs[count + group :]
    _, _, chunk, _ = pool.shape
    at = 0
    for k, cut in enumerate(cuts):
        label_buf[k : k + 1, :] = parts[at][-LABEL_ROWS:, :].astype(jnp.float32)[:1].astype(jnp.int32)
        at += cut
    copy = pltpu.make_async_copy(label_buf, label_ref, sem)
    copy.start()
    at = 0
    for k, cut in enumerate(cuts):
        first = 0
        for part in parts[at : at + cut]:
            span = part.shape[0] // (blocks * chunk)
            for b in range(blocks):
                for tile in range(span):
                    row = (b * span + tile) * chunk
                    pool[k * blocks + b, first + tile] = part[row : row + chunk, :]
            first += span
        at += cut
    nothing = len(cuts) * blocks
    pool[nothing] = jnp.zeros(pool.shape[1:], pool.dtype)
    wanted = group * SLOTS
    for i in range(wanted):
        table[i] = nothing
    copy.wait()
    own_index = lax.axis_index("seq")
    for k in range(len(cuts)):
        for b in range(blocks):
            member = label_ref[k, 2 * b] ^ own_index
            slot = label_ref[k, 2 * b + 1]
            table[jnp.where(member < group, member * SLOTS + slot, wanted)] = k * blocks + b
    for m in range(group):
        for s in range(SLOTS):
            outs[m][s] = pool[table[m * SLOTS + s]]


def route(parts, group, blocks):
    cuts = tuple(len(part) for part in parts)
    flat = [near(array) for part in parts for array in part]
    chunk = BLOCK // group
    tiles = (parts[0][0].shape[0] - LABEL_ROWS) // (blocks * chunk)
    count = len(cuts)
    return pl.pallas_call(
        functools.partial(route_kernel, cuts, group, blocks),
        in_specs=[VMEM] * len(flat),
        out_specs=[VMEM] * group,
        out_shape=[pltpu.VMEM((SLOTS, tiles, chunk, 128), jnp.bfloat16)] * group,
        scratch_shapes=[
            pltpu.VMEM((count * blocks + 1, tiles, chunk, 128), jnp.bfloat16),
            pltpu.VMEM((count, 128), jnp.int32),
            pltpu.SMEM((count, 128), jnp.int32),
            pltpu.SMEM((group * SLOTS + 1,), jnp.int32),
            pltpu.SemaphoreType.DMA,
        ],
        compiler_params=pltpu.CompilerParams(vmem_limit_bytes=VMEM_LIMIT),
        cost_estimate=pl.CostEstimate(
            flops=0,
            bytes_accessed=256 * (count * blocks + group * SLOTS) * tiles * chunk,
            transcendentals=0,
        ),
        name="route",
    )(*flat)


def join_kernel(members, *refs):
    out, sems = refs[-2:]
    parts = refs[: len(members)]
    _, tiles, chunk, _ = parts[0].shape
    own = lax.rem(lax.axis_index("seq"), BLOCK // chunk)
    copies = []
    for at, m in enumerate(members):
        start = pl.multiple_of((own ^ m) * chunk, chunk)
        for tile in range(tiles):
            there = out.at[:, pl.ds(start, chunk), tile * 128 : (tile + 1) * 128]
            copy = pltpu.make_async_copy(parts[at].at[:, tile], there, sems.at[at, tile])
            copy.start()
            copies.append(copy)
    for copy in copies:
        copy.wait()


def join(parts, members, before=None):
    slots, tiles, chunk, _ = parts[0].shape
    cols = tiles * 128
    operands = [near(part) for part in parts]
    in_specs = [VMEM] * len(parts)
    alias = {}
    if before is not None:
        operands.append(before)
        in_specs.append(ANY)
        alias = {len(parts): 0}
    return pl.pallas_call(
        functools.partial(join_kernel, members),
        in_specs=in_specs,
        out_specs=ANY,
        out_shape=jax.ShapeDtypeStruct((slots, BLOCK, cols), jnp.bfloat16),
        scratch_shapes=[pltpu.SemaphoreType.DMA((len(parts), tiles))],
        input_output_aliases=alias,
        compiler_params=pltpu.CompilerParams(vmem_limit_bytes=VMEM_LIMIT),
        cost_estimate=pl.CostEstimate(
            flops=0, bytes_accessed=4 * len(parts) * slots * chunk * cols, transcendentals=0
        ),
        name="join" if before is None else "join_last",
    )(*operands)


def per_device(seq_size, hidden, norm_gain, w_kv, lengths, page_table):
    seq_count, row_count, local_width = hidden.shape
    group = min(4, seq_size)
    flat = hidden.reshape(seq_count * row_count, local_width)
    other = lax.ppermute(flat, "tensor", [(0, 1), (1, 0)])

    def swap(array, k):
        return lax.ppermute(array, "seq", [(i, i ^ k) for i in range(seq_size)])

    gain = norm_gain.reshape(-1, 128)
    pages = page_table.reshape(-1)
    freq = frequencies()
    flat, freq = lax.optimization_barrier((flat, freq))
    acc, squares, far, gain, cosine, sine = first_half(flat, gain, w_kv, freq, row_count)
    shared = (cosine, sine, group)
    early, before, inv = second_half(lengths, pages, other, gain, far, acc, squares, *shared)
    parts = {k: [] for k in range(seq_size)}

    def send(array, k):
        parts[k].append(swap(array, k))

    if seq_size > group:
        send(early, group)
    late, *outs = second_half(lengths, pages, other, gain, far, acc, inv, *shared, before)
    if seq_size > group:
        send(late, group)
    for k in range(1, seq_size):
        if k != group:
            send(outs[k % group], k)
    parts[0] = [outs[0]]
    sent = route([parts[k] for k in range(seq_size)], group, seq_count * row_count // BLOCK)
    placed = [sent[0]]
    for m in range(1, group):
        placed.append(swap(sent[m], m))
    members = tuple(range(group))
    kv_cache = join(placed[:-1], members[:-1])
    return join(placed[-1:], members[-1:], kv_cache)


def solution(mesh):
    placed = (P("group", "seq", "tensor"), P(), P(None, "tensor"), P("group"), P("group", "seq"))

    def body(*operands):
        return per_device(mesh.shape["seq"], *operands)

    return jax.shard_map(
        body,
        mesh=mesh,
        in_specs=placed,
        out_specs=P(("group", "seq"), None, "tensor"),
        check_vma=False,
    )
```

time: 53.7 us -> 53.3 us (level)
  Pallas kernels: 10.4 us -> 11 us
    ppermute x11, waiting for transfers between devices: 24 us -> 23.1 us  [swap(): return lax.ppermute(array, 'seq', [(i, i ^ k) for i in range(seq_size)])]
    pallas_call x2 -> x3, Pallas kernels: 6.05 us -> 6.71 us  [the longest x1 5.01 us: first_half(): pl.pallas_call(functools.partial(first_half_kernel, row_count), in_specs=...]
  transfers between devices with their start and end apart: 12 -> 12, of which waited for: 6 -> 7; matrix products, arithmetic and copies ran while one was open for 1% -> 0% of each run, Pallas kernels for 9% -> 11%
where the time goes in v1:
time: 53.3 us; the launch traced here: 53.1 us
  waiting for transfers between devices  23.5 us (44%)
  starting transfers between devices  18.6 us (35%)
  Pallas kernels  11 us (21%)
    ppermute x11, waiting for transfers between devices, swap(): return lax.ppermute(array, 'seq', [(i, i ^ k) for i in range(seq_size)])  23.1 us
    ppermute x11, starting transfers between devices, swap(): return lax.ppermute(array, 'seq', [(i, i ^ k) for i in range(seq_size)])  18.1 us
    pallas_call x1, Pallas kernels, first_half(): pl.pallas_call(functools.partial(first_half_kernel, row_count), in_specs=...  5.01 us
    pallas_call x2, Pallas kernels, second_half(): pl.pallas_call(functools.partial(second_half_kernel, group, piece), in_sp...  3.51 us
    pallas_call x2, Pallas kernels, join(): pl.pallas_call(functools.partial(join_kernel, members), in_specs=in_specs...  1.69 us
  transfers between devices with their start and end apart: 12, of which 7 were waited for; matrix products, arithmetic and copies ran while one was open for 0% of the time, Pallas kernels for 11%

profile of v1, /device:TPU:0, one launch (start us, length us, event | category | flops | bytes accessed | tf_op | source)
XLA Modules:
  0.0 53.1 jit_solution(12854503776173450183)
XLA Ops:
  0.0 0.5 collective-permute-start
  0.5 0.0 copy-start.1
  0.5 5.0 %first_half.1 = (f32[384,512]{1,0:T(8,128)S(1)}, f32[384,128]{1,0:T(8,128)S(1)}, bf16[4096,512]{1,0:T(8,128)(2,1)S(1)}, f32[64,128]{1,0:T(8,128)S(1)}, f32[128,128]{1,0:T(8,128)S(1)}, /*index=5*/f32[128,128]{1,0:T(8,128)S(1)}) custom-call(bf16[384,4096]{1,0:T(8,128)(2,1)} %bitcast.6, bf16[64,128]{1,0:T(8,128)(2,1)} %bitcast.7, bf16[8192,512]{1,0:T(8,128)(2,1)} %w_hbm.1, ...), custom_call_target="tpu_custom_call" | custom-call | flops 1610612736 | bytes 12320768 | tf_op jit(solution)/shard_map/first_half/pallas_call | solution.py:116
  5.5 0.5 collective-permute-done.x_ref
  6.0 1.8 %shard_map.55 = (bf16[200,128]{1,0:T(8,128)(2,1)S(1)}, bf16[3,2,128,128]{3,2,1,0:T(8,128)(2,1)S(1)}, f32[384,128]{1,0:T(8,128)S(1)}) custom-call(s32[3]{0:T(128)S(1)} %copy-done, s32[3]{0:T(128)S(1)} %bitcast.3, bf16[384,4096]{1,0:T(8,128)(2,1)S(1)} %collective-permute-done.x_ref, f32[64,128]{1,0:T(8,128)S(1)} %get-tuple-element.27.g_ref, ...), custom_call_target="tpu_custom_call" | custom-call | flops 805306368 | bytes 5636096 | tf_op jit(solution)/shard_map/pallas_call | solution.py:239
  7.8 1.7 %shard_map.56 = (bf16[192,128]{1,0:T(8,128)(2,1)S(1)}, bf16[392,128]{1,0:T(8,128)(2,1)S(1)}, bf16[392,128]{1,0:T(8,128)(2,1)S(1)}, bf16[392,128]{1,0:T(8,128)(2,1)S(1)}, bf16[392,128]{1,0:T(8,128)(2,1)S(1)}) custom-call(s32[3]{0:T(128)S(1)} %copy-done, s32[3]{0:T(128)S(1)} %bitcast.4, bf16[384,4096]{1,0:T(8,128)(2,1)S(1)} %collective-permute-done.x_ref, ...), custom_call_target="tpu_custom_call" | custom-call | flops 805306368 | bytes 5636096 | tf_op jit(solution)/shard_map/pallas_call | solution.py:239
  9.5 5.0 %collective-permute-start.6 = (bf16[392,128]{1,0:T(8,128)(2,1)S(1)}, bf16[392,128]{1,0:T(8,128)(2,1)S(1)}, u32[]{:S(2)}, u32[]{:S(2)}) collective-permute-start(bf16[392,128]{1,0:T(8,128)(2,1)S(1)} %get-tuple-element.36), channel_id=1, source_target_pairs={{0,10},{2,8},{4,14},{6,12},{8,2},{10,0},{12,6},{14,4},{1,11},{3,9}... | collective-permute-start | bytes 301064 | tf_op jit(solution)/shard_map/ppermute | solution.py:371
  14.5 0.3 collective-permute-start.4
  14.8 2.6 %collective-permute-start.5 = (bf16[192,128]{1,0:T(8,128)(2,1)S(1)}, bf16[192,128]{1,0:T(8,128)(2,1)S(1)}, u32[]{:S(2)}, u32[]{:S(2)}) collective-permute-start(bf16[192,128]{1,0:T(8,128)(2,1)S(1)} %get-tuple-element.40), channel_id=1, source_target_pairs={{0,8},{2,10},{4,12},{6,14},{8,0},{10,2},{12,4},{14,6},{1,9},{3,11}... | collective-permute-start | bytes 147464 | tf_op jit(solution)/shard_map/ppermute | solution.py:371
  17.4 0.5 collective-permute-start.1
  17.9 1.3 %collective-permute-start.7 = (bf16[392,128]{1,0:T(8,128)(2,1)S(1)}, bf16[392,128]{1,0:T(8,128)(2,1)S(1)}, u32[]{:S(2)}, u32[]{:S(2)}) collective-permute-start(bf16[392,128]{1,0:T(8,128)(2,1)S(1)} %get-tuple-element.37), channel_id=1, source_target_pairs={{0,12},{2,14},{4,8},{6,10},{8,4},{10,6},{12,0},{14,2},{1,13},{3,15... | collective-permute-start | bytes 301064 | tf_op jit(solution)/shard_map/ppermute | solution.py:371
  19.3 7.8 %collective-permute-done.5.refs_5_ = bf16[192,128]{1,0:T(8,128)(2,1)S(1)} collective-permute-done((bf16[192,128]{1,0:T(8,128)(2,1)S(1)}, bf16[192,128]{1,0:T(8,128)(2,1)S(1)}, u32[]{:S(2)}, u32[]{:S(2)}) %collective-permute-start.5) | collective-permute-done | bytes 49184 | tf_op jit(solution)/shard_map/ppermute | solution.py:371
  27.1 2.7 %collective-permute-start.8 = (bf16[392,128]{1,0:T(8,128)(2,1)S(1)}, bf16[392,128]{1,0:T(8,128)(2,1)S(1)}, u32[]{:S(2)}, u32[]{:S(2)}) collective-permute-start(bf16[392,128]{1,0:T(8,128)(2,1)S(1)} %get-tuple-element.38), channel_id=1, source_target_pairs={{0,14},{2,12},{4,10},{6,8},{8,6},{10,4},{12,2},{14,0},{1,15},{3,13... | collective-permute-start | bytes 301064 | tf_op jit(solution)/shard_map/ppermute | solution.py:371
  29.8 2.1 %collective-permute-start.3 = (bf16[392,128]{1,0:T(8,128)(2,1)S(1)}, bf16[392,128]{1,0:T(8,128)(2,1)S(1)}, u32[]{:S(2)}, u32[]{:S(2)}) collective-permute-start(bf16[392,128]{1,0:T(8,128)(2,1)S(1)} %get-tuple-element.38), channel_id=1, source_target_pairs={{0,6},{2,4},{4,2},{6,0},{8,14},{10,12},{12,10},{14,8},{1,7},{3,5},... | collective-permute-start | bytes 301064 | tf_op jit(solution)/shard_map/ppermute | solution.py:371
  31.9 3.7 %collective-permute-done.8.refs_8_ = bf16[392,128]{1,0:T(8,128)(2,1)S(1)} collective-permute-done((bf16[392,128]{1,0:T(8,128)(2,1)S(1)}, bf16[392,128]{1,0:T(8,128)(2,1)S(1)}, u32[]{:S(2)}, u32[]{:S(2)}) %collective-permute-start.8) | collective-permute-done | bytes 100384 | tf_op jit(solution)/shard_map/ppermute | solution.py:371
  35.6 1.2 %collective-permute-done.3.refs_3_ = bf16[392,128]{1,0:T(8,128)(2,1)S(1)} collective-permute-done((bf16[392,128]{1,0:T(8,128)(2,1)S(1)}, bf16[392,128]{1,0:T(8,128)(2,1)S(1)}, u32[]{:S(2)}, u32[]{:S(2)}) %collective-permute-start.3) | collective-permute-done | bytes 100384 | tf_op jit(solution)/shard_map/ppermute | solution.py:371
  36.8 0.8 %route.1 = (bf16[8,4,32,128]{3,2,1,0:T(8,128)(2,1)S(1)}, bf16[8,4,32,128]{3,2,1,0:T(8,128)(2,1)S(1)}, bf16[8,4,32,128]{3,2,1,0:T(8,128)(2,1)S(1)}, bf16[8,4,32,128]{3,2,1,0:T(8,128)(2,1)S(1)}) custom-call(bf16[392,128]{1,0:T(8,128)(2,1)S(1)} %get-tuple-element.35.refs_0_, bf16[392,128]{1,0:T(8,128)(2,1)S(1)} %collective-permute-done.1.refs_1_, ...), custom_call_target="tpu_custom_call" | custom-call | bytes 1835008 | tf_op jit(solution)/shard_map/route/pallas_call | solution.py:300
  37.6 1.6 %collective-permute-start.10 = (bf16[8,4,32,128]{3,2,1,0:T(8,128)(2,1)S(1)}, bf16[8,4,32,128]{3,2,1,0:T(8,128)(2,1)S(1)}, u32[]{:S(2)}, u32[]{:S(2)}) collective-permute-start(bf16[8,4,32,128]{3,2,1,0:T(8,128)(2,1)S(1)} %get-tuple-element.43), channel_id=1, source_target_pairs={{0,2},{2,0},{4,6},{6,4},{8,10},{10,8},{12,14},{14,12},{1,3},{3,1},... | collective-permute-start | bytes 786440 | tf_op jit(solution)/shard_map/ppermute | solution.py:371
  39.2 2.0 %collective-permute-start.9 = (bf16[8,4,32,128]{3,2,1,0:T(8,128)(2,1)S(1)}, bf16[8,4,32,128]{3,2,1,0:T(8,128)(2,1)S(1)}, u32[]{:S(2)}, u32[]{:S(2)}) collective-permute-start(bf16[8,4,32,128]{3,2,1,0:T(8,128)(2,1)S(1)} %get-tuple-element.41), channel_id=1, source_target_pairs={{0,6},{2,4},{4,2},{6,0},{8,14},{10,12},{12,10},{14,8},{1,7},{3,5},... | collective-permute-start | bytes 786440 | tf_op jit(solution)/shard_map/ppermute | solution.py:371
  41.1 4.8 %collective-permute-done.10.refs_1_ = bf16[8,4,32,128]{3,2,1,0:T(8,128)(2,1)S(1)} collective-permute-done((bf16[8,4,32,128]{3,2,1,0:T(8,128)(2,1)S(1)}, bf16[8,4,32,128]{3,2,1,0:T(8,128)(2,1)S(1)}, u32[]{:S(2)}, u32[]{:S(2)}) %collective-permute-start.10) | collective-permute-done | bytes 262176 | tf_op jit(solution)/shard_map/ppermute | solution.py:371
  45.9 2.4 %collective-permute-done.11.refs_2_ = bf16[8,4,32,128]{3,2,1,0:T(8,128)(2,1)S(1)} collective-permute-done((bf16[8,4,32,128]{3,2,1,0:T(8,128)(2,1)S(1)}, bf16[8,4,32,128]{3,2,1,0:T(8,128)(2,1)S(1)}, u32[]{:S(2)}, u32[]{:S(2)}) %collective-permute-start.11) | collective-permute-done | bytes 262176 | tf_op jit(solution)/shard_map/ppermute | solution.py:371
  48.3 1.0 %join.1.refs_1_ = bf16[8,128,512]{2,1,0:T(8,128)(2,1)} custom-call(bf16[8,4,32,128]{3,2,1,0:T(8,128)(2,1)S(1)} %get-tuple-element.42.refs_0_, bf16[8,4,32,128]{3,2,1,0:T(8,128)(2,1)S(1)} %collective-permute-done.10.refs_1_, bf16[8,4,32,128]{3,2,1,0:T(8,128)(2,1)S(1)} %collective-permute-done.11.refs_2_), custom_call_target="tpu_custom_call" | custom-call | bytes 1572864 | tf_op jit(solution)/shard_map/join/pallas_call | solution.py:349
  49.3 3.1 %collective-permute-done.9.refs_0_ = bf16[8,4,32,128]{3,2,1,0:T(8,128)(2,1)S(1)} collective-permute-done((bf16[8,4,32,128]{3,2,1,0:T(8,128)(2,1)S(1)}, bf16[8,4,32,128]{3,2,1,0:T(8,128)(2,1)S(1)}, u32[]{:S(2)}, u32[]{:S(2)}) %collective-permute-start.9) | collective-permute-done | bytes 262176 | tf_op jit(solution)/shard_map/ppermute | solution.py:371
  52.4 0.7 %join_last.1 = bf16[8,128,512]{2,1,0:T(8,128)(2,1)} custom-call(bf16[8,4,32,128]{3,2,1,0:T(8,128)(2,1)S(1)} %collective-permute-done.9.refs_0_, bf16[8,128,512]{2,1,0:T(8,128)(2,1)} %join.1.refs_1_), custom_call_target="tpu_custom_call", output_to_operand_aliasing={{}: (1, {})} | custom-call | bytes 524288 | tf_op jit(solution)/shard_map/join_last/pallas_call | solution.py:349
  (11 shorter events, 0.0 us)
Async XLA Ops:
  0.0 6.0 %collective-permute-start = (bf16[384,4096]{1,0:T(8,128)(2,1)}, bf16[384,4096]{1,0:T(8,128)(2,1)S(1)}, u32[]{:S(2)}, u32[]{:S(2)}) collective-permute-start(bf16[384,4096]{1,0:T(8,128)(2,1)} %bitcast.5), channel_id=1, source_target_pairs={{0,1},{1,0},{2,3},{3,2},{4,5},{5,4},{6,7},{7,6},{8,9},{9,8},{10,11... | collective-permute-start | bytes 9437192 | tf_op jit(solution)/shard_map/ppermute | solution.py:368
  0.5 5.5 %copy-start = (s32[3]{0:T(128)S(1)}, s32[3]{0:T(128)}, u32[]{:S(2)}) copy-start(s32[3]{0:T(128)} %len_ref.3) | copy-start | bytes 40
  0.5 5.5 %copy-start.1 = (s32[3,1]{0,1:T(1,128)S(1)}, s32[3,1]{0,1:T(1,128)}, u32[]{:S(2)}) copy-start(s32[3,1]{0,1:T(1,128)} %param.9) | copy-start | bytes 40
  9.5 20.3 %collective-permute-start.6 = (bf16[392,128]{1,0:T(8,128)(2,1)S(1)}, bf16[392,128]{1,0:T(8,128)(2,1)S(1)}, u32[]{:S(2)}, u32[]{:S(2)}) collective-permute-start(bf16[392,128]{1,0:T(8,128)(2,1)S(1)} %get-tuple-element.36), channel_id=1, source_target_pairs={{0,10},{2,8},{4,14},{6,12},{8,2},{10,0},{12,6},{14,4},{1,11},{3,9}... | collective-permute-start | bytes 301064 | tf_op jit(solution)/shard_map/ppermute | solution.py:371
  14.5 12.6 %collective-permute-start.4 = (bf16[200,128]{1,0:T(8,128)(2,1)S(1)}, bf16[200,128]{1,0:T(8,128)(2,1)S(1)}, u32[]{:S(2)}, u32[]{:S(2)}) collective-permute-start(bf16[200,128]{1,0:T(8,128)(2,1)S(1)} %get-tuple-element.39), channel_id=1, source_target_pairs={{0,8},{2,10},{4,12},{6,14},{8,0},{10,2},{12,4},{14,6},{1,9},{3,11}... | collective-permute-start | bytes 153608 | tf_op jit(solution)/shard_map/ppermute | solution.py:371
  14.8 12.3 %collective-permute-start.5 = (bf16[192,128]{1,0:T(8,128)(2,1)S(1)}, bf16[192,128]{1,0:T(8,128)(2,1)S(1)}, u32[]{:S(2)}, u32[]{:S(2)}) collective-permute-start(bf16[192,128]{1,0:T(8,128)(2,1)S(1)} %get-tuple-element.40), channel_id=1, source_target_pairs={{0,8},{2,10},{4,12},{6,14},{8,0},{10,2},{12,4},{14,6},{1,9},{3,11}... | collective-permute-start | bytes 147464 | tf_op jit(solution)/shard_map/ppermute | solution.py:371
  17.4 14.5 %collective-permute-start.1 = (bf16[392,128]{1,0:T(8,128)(2,1)S(1)}, bf16[392,128]{1,0:T(8,128)(2,1)S(1)}, u32[]{:S(2)}, u32[]{:S(2)}) collective-permute-start(bf16[392,128]{1,0:T(8,128)(2,1)S(1)} %get-tuple-element.36), channel_id=1, source_target_pairs={{0,2},{2,0},{4,6},{6,4},{8,10},{10,8},{12,14},{14,12},{1,3},{3,1},... | collective-permute-start | bytes 301064 | tf_op jit(solution)/shard_map/ppermute | solution.py:371
  17.9 14.0 %collective-permute-start.7 = (bf16[392,128]{1,0:T(8,128)(2,1)S(1)}, bf16[392,128]{1,0:T(8,128)(2,1)S(1)}, u32[]{:S(2)}, u32[]{:S(2)}) collective-permute-start(bf16[392,128]{1,0:T(8,128)(2,1)S(1)} %get-tuple-element.37), channel_id=1, source_target_pairs={{0,12},{2,14},{4,8},{6,10},{8,4},{10,6},{12,0},{14,2},{1,13},{3,15... | collective-permute-start | bytes 301064 | tf_op jit(solution)/shard_map/ppermute | solution.py:371
  27.1 4.8 %collective-permute-start.2 = (bf16[392,128]{1,0:T(8,128)(2,1)S(1)}, bf16[392,128]{1,0:T(8,128)(2,1)S(1)}, u32[]{:S(2)}, u32[]{:S(2)}) collective-permute-start(bf16[392,128]{1,0:T(8,128)(2,1)S(1)} %get-tuple-element.37), channel_id=1, source_target_pairs={{0,4},{2,6},{4,0},{6,2},{8,12},{10,14},{12,8},{14,10},{1,5},{3,7},... | collective-permute-start | bytes 301064 | tf_op jit(solution)/shard_map/ppermute | solution.py:371
  27.1 8.5 %collective-permute-start.8 = (bf16[392,128]{1,0:T(8,128)(2,1)S(1)}, bf16[392,128]{1,0:T(8,128)(2,1)S(1)}, u32[]{:S(2)}, u32[]{:S(2)}) collective-permute-start(bf16[392,128]{1,0:T(8,128)(2,1)S(1)} %get-tuple-element.38), channel_id=1, source_target_pairs={{0,14},{2,12},{4,10},{6,8},{8,6},{10,4},{12,2},{14,0},{1,15},{3,13... | collective-permute-start | bytes 301064 | tf_op jit(solution)/shard_map/ppermute | solution.py:371
  29.8 7.0 %collective-permute-start.3 = (bf16[392,128]{1,0:T(8,128)(2,1)S(1)}, bf16[392,128]{1,0:T(8,128)(2,1)S(1)}, u32[]{:S(2)}, u32[]{:S(2)}) collective-permute-start(bf16[392,128]{1,0:T(8,128)(2,1)S(1)} %get-tuple-element.38), channel_id=1, source_target_pairs={{0,6},{2,4},{4,2},{6,0},{8,14},{10,12},{12,10},{14,8},{1,7},{3,5},... | collective-permute-start | bytes 301064 | tf_op jit(solution)/shard_map/ppermute | solution.py:371
  37.6 8.3 %collective-permute-start.10 = (bf16[8,4,32,128]{3,2,1,0:T(8,128)(2,1)S(1)}, bf16[8,4,32,128]{3,2,1,0:T(8,128)(2,1)S(1)}, u32[]{:S(2)}, u32[]{:S(2)}) collective-permute-start(bf16[8,4,32,128]{3,2,1,0:T(8,128)(2,1)S(1)} %get-tuple-element.43), channel_id=1, source_target_pairs={{0,2},{2,0},{4,6},{6,4},{8,10},{10,8},{12,14},{14,12},{1,3},{3,1},... | collective-permute-start | bytes 786440 | tf_op jit(solution)/shard_map/ppermute | solution.py:371
  39.2 9.2 %collective-permute-start.11 = (bf16[8,4,32,128]{3,2,1,0:T(8,128)(2,1)S(1)}, bf16[8,4,32,128]{3,2,1,0:T(8,128)(2,1)S(1)}, u32[]{:S(2)}, u32[]{:S(2)}) collective-permute-start(bf16[8,4,32,128]{3,2,1,0:T(8,128)(2,1)S(1)} %get-tuple-element.44), channel_id=1, source_target_pairs={{0,4},{2,6},{4,0},{6,2},{8,12},{10,14},{12,8},{14,10},{1,5},{3,7},... | collective-permute-start | bytes 786440 | tf_op jit(solution)/shard_map/ppermute | solution.py:371
  39.2 13.2 %collective-permute-start.9 = (bf16[8,4,32,128]{3,2,1,0:T(8,128)(2,1)S(1)}, bf16[8,4,32,128]{3,2,1,0:T(8,128)(2,1)S(1)}, u32[]{:S(2)}, u32[]{:S(2)}) collective-permute-start(bf16[8,4,32,128]{3,2,1,0:T(8,128)(2,1)S(1)} %get-tuple-element.41), channel_id=1, source_target_pairs={{0,6},{2,4},{4,2},{6,0},{8,14},{10,12},{12,10},{14,8},{1,7},{3,5},... | collective-permute-start | bytes 786440 | tf_op jit(solution)/shard_map/ppermute | solution.py:371
